TPU v7x, 256 devices: a whole 4x4x8 slice. The times are simulated.
256 devices in a mesh: proc: 32 (over x, z), rep: 8 (over y, core).
Axes of the slice: x: 4, y: 4, z: 8, core: 2. Of those that a mesh axis runs over, the one named last changes fastest.
Arguments:
- amplitudes: bfloat16 [512, 208, 128], P('proc'), may hold values from -6 to 6
- ladder_rows: int32 [512, 8, 14], P('proc', 'rep'), may hold values from -1 to 511, as said below
- ladder_ints: bfloat16 [512, 8, 14, 128, 128], P('proc', 'rep'), may hold values from -0.046875 to 0.046875
- cycle_rows: int32 [512, 8, 8], P('proc', 'rep'), may hold values from 0 to 511, as said below
- cycle_ints: bfloat16 [512, 8, 8, 128, 128], P('proc', 'rep'), may hold values from -0.0625 to 0.0625
- bare_ints: bfloat16 [512, 208, 128], P('proc', 'rep'), may hold values from -6 to 6
- occ_energy: float32 [8, 208], replicated, may hold values from -2 to -0.5
- vir_energy: float32 [512, 128], P('proc'), may hold values from 0.5 to 4
- block_tiles: int32 [8], replicated, may hold values from 8 to 112, as said below
Outputs:
- new_amplitudes: bfloat16 [512, 208, 128], P('proc', 'rep')
Inputs may be any that keep to these rules, and one draw needn't show every extreme that they name: `block_tiles`: each entry is a multiple of 8; the entries sum to 512; the irreps' tiles lie one after another in irrep order; one irrep has 112 tiles. `ladder_rows`: for a column tile l of irrep g and an index r of the second dimension, the entries list, in some order, every tile k of irrep g with k % 8 == r once; the other entries are -1. The columns of the largest irrep fill all 14 entries. `cycle_rows`: every entry at index r of the second dimension is a tile k with k % 8 == r; entries may repeat.
All inputs are finite; a program needn't handle non-finite values.
Results may differ from a plain program's by a relative error of at most 0.001.
Values may be sent and summed in bfloat16 or wider, within the bound.
No kernel may reach another device: no remote copies, remote signals or barrier semaphores. Data moves between devices by JAX's collectives and lax.ppermute only.
A program may use at most 128 MiB of HBM per device.

v0:
```python
import jax
import jax.numpy as jnp
from jax import lax
from jax.sharding import PartitionSpec as P


def local(
    amplitudes,
    ladder_rows,
    ladder_ints,
    cycle_rows,
    cycle_ints,
    bare_ints,
    occ_energy,
    vir_energy,
    block_tiles,
):
    copies = lax.axis_size("rep")
    replica = lax.axis_index("rep")
    proc_index = lax.axis_index("proc")
    tiles_dev, pair_rows, tile_width = amplitudes.shape
    gathered = lax.all_gather(amplitudes, "proc", axis=0, tiled=True)
    ladder_list = ladder_rows[:, 0, :]
    usable = ladder_list >= 0
    ladder_tiles = gathered[jnp.maximum(ladder_list, 0)]
    ladder_tiles = jnp.where(
        usable[:, :, None, None], ladder_tiles, jnp.zeros((), ladder_tiles.dtype)
    )
    partial_value = jnp.einsum(
        "lsrk,lskc->lrc", ladder_tiles, ladder_ints[:, 0], preferred_element_type=jnp.float32
    )
    cycle_tiles = gathered[cycle_rows[:, 0, :]]
    partial_value = partial_value + jnp.einsum(
        "lsrk,lskc->lrc", cycle_tiles, cycle_ints[:, 0], preferred_element_type=jnp.float32
    )
    row_share = pair_rows // copies
    summed = lax.psum_scatter(partial_value, "rep", scatter_dimension=1, tiled=True)
    residual = bare_ints.astype(jnp.float32) + summed
    columns = proc_index * tiles_dev + jnp.arange(tiles_dev, dtype=jnp.int32)
    bounds = jnp.cumsum(block_tiles)
    irreps = jnp.sum((columns[:, None] >= bounds[None, :]).astype(jnp.int32), axis=1)
    selector = (
        irreps[:, None] == jnp.arange(block_tiles.shape[0], dtype=jnp.int32)[None, :]
    ).astype(jnp.float32)
    occ_rows = jnp.dot(selector, occ_energy, precision=lax.Precision.HIGHEST)
    occ_mine = lax.dynamic_slice_in_dim(occ_rows, replica * row_share, row_share, 1)
    denominator = vir_energy[:, None, :] - occ_mine[:, :, None]
    return (residual / denominator).astype(jnp.bfloat16)


def solution(mesh):
    return jax.shard_map(
        local,
        mesh=mesh,
        in_specs=(
            P("proc", None, None),
            P("proc", "rep", None),
            P("proc", "rep", None, None, None),
            P("proc", "rep", None),
            P("proc", "rep", None, None, None),
            P("proc", "rep", None),
            P(),
            P("proc", None),
            P(),
        ),
        out_specs=P("proc", "rep", None),
        check_vma=False,
    )
```

profile of v0, /device:TPU:2, one launch (start us, length us, event | category | flops | bytes accessed | tf_op | source)
XLA Modules:
  0.0 300.1 jit_solution(15536035518188840709)
XLA Ops:
  6.5 0.0 copy-start
  6.5 0.0 all-gather.2.cloned.1.call-start
  6.5 0.7 all-gather.2.cloned.1.call-update
  7.3 0.0 reduce-scatter.2.cloned.1.call-start
  7.3 0.7 compare_select_fusion
  8.0 0.1 copy.26
  8.1 0.1 reshape.90
  8.2 0.7 broadcast_maximum_fusion
  8.9 0.1 copy.25
  9.0 0.1 reshape.82
  9.0 0.7 broadcast_compare_fusion
  9.8 0.1 copy.31
  9.9 197.5 %all-gather.2.cloned.1.call-done = bf16[512,208,128]{2,1,0:T(8,128)(2,1)} async-done(((bf16[16,208,128]{2,1,0:T(8,128)(2,1)}), bf16[512,208,128]{2,1,0:T(8,128)(2,1)}) %all-gather.2.cloned.1.call-update) | async-done | bytes 27262992 | tf_op jit(solution)/shard_map/all_gather | solution.py:22
  207.4 12.9 %gather_fusion.1 = bf16[128,208,128]{2,1,0:T(8,128)(2,1)} fusion(bf16[512,208,128]{2,1,0:T(8,128)(2,1)} %all-gather.2.cloned.1.call-done, s32[1024]{0:T(1024)S(1)} %pad_clamp_fusion), kind=kCustom, calls=%fused_computation.1 | custom fusion | bytes 13632000 | tf_op jit(solution)/shard_map/gather | solution.py:32
  220.3 6.1 %fusion.5 = f32[16,208,128,1]{2,1,3,0:T(8,128)S(1)} fusion(bf16[16,8,208,128]{3,2,1,0:T(8,128)(2,1)} %bitcast.27, bf16[16,1,8,128,128]{4,3,2,1,0:T(8,128)(2,1)} %param.13), kind=kOutput, calls=%fused_computation.7 | convolution fusion | flops 872415232 | bytes 12713984 | tf_op jit(solution)/shard_map/lsrk,lskc->lrc/dot_general | solution.py:33
  226.4 19.3 %gather_fusion = bf16[224,208,128]{2,1,0:T(8,128)(2,1)} fusion(bf16[512,208,128]{2,1,0:T(8,128)(2,1)} %all-gather.2.cloned.1.call-done, s32[1024]{0:T(1024)S(1)} %pad_clamp_fusion.1), kind=kCustom, calls=%fused_computation | custom fusion | bytes 23856000 | tf_op jit(solution)/shard_map/gather | solution.py:25
  245.7 0.0 copy-start.3
  245.7 0.0 copy-start.1
  245.7 0.0 copy-start.2
  245.7 9.9 %bitcast_add_fusion = f32[16,208,128]{2,1,0:T(8,128)S(1)} fusion(f32[16,208,128,1]{2,1,3,0:T(8,128)S(1)} %fusion.5, bf16[16,1,14,128,128]{4,3,2,1,0:T(8,128)(2,1)} %param.11, bf16[16,14,208,128]{3,2,1,0:T(8,128)(2,1)} %bitcast.28, pred[16,14]{1,0:T(8,128)(4,1)S(1)} %bitcast.29), kind=kOutput, calls=%fused_computation.9 | convolution fusion | flops 1533116416 | bytes 22675680 | tf_op jit(solution)/shard_map/lsrk,lskc->lrc/dot_general | solution.py:29
  255.6 1.7 copy.27
  257.3 0.0 reduce-scatter.2.cloned.1.call-update
  257.3 0.0 copy-done.3
  257.3 0.2 reduce-window.8
  257.5 0.1 convert_reduce_fusion
  257.6 0.0 copy-done
  257.6 0.2 fusion.11
  257.8 0.1 constant_dynamic-slice_fusion
  257.9 0.1 copy.28
  258.0 33.6 %reduce-scatter.2.cloned.1.call-done = f32[16,26,128]{2,0,1:T(8,128)} async-done(((f32[16,208,128]{2,0,1:T(8,128)}), f32[16,26,128]{2,0,1:T(8,128)}) %reduce-scatter.2.cloned.1.call-update) | async-done | bytes 213008 | tf_op jit(solution)/shard_map/reduce_scatter | solution.py:37
  291.6 0.0 copy-done.1
  291.6 0.0 copy-done.2
  291.6 1.7 divide_convert_fusion
  (3 shorter events, 0.0 us)
Async XLA Ops:
  6.5 251.1 %copy-start = (f32[8,208]{1,0:T(8,128)S(1)}, f32[8,208]{1,0:T(8,128)}, u32[]{:S(2)}) copy-start(f32[8,208]{1,0:T(8,128)} %param.15) | copy-start | bytes 19972
  6.5 200.9 %all-gather.2.cloned.1.call-start = ((), (), s32[]{:S(2)}) async-start(), calls=%async_computation.1 | async-start | bytes 28114944 | tf_op jit(solution)/shard_map/all_gather | solution.py:22
  7.3 284.3 %reduce-scatter.2.cloned.1.call-start = ((), (), s32[]{:S(2)}) async-start(), calls=%async_computation.2 | async-start | bytes 1916928 | tf_op jit(solution)/shard_map/reduce_scatter | solution.py:37
  245.7 11.6 %copy-start.3 = (s32[8]{0:T(128)S(1)}, s32[8]{0:T(128)}, u32[]{:S(2)}) copy-start(s32[8]{0:T(128)} %param.17) | copy-start | bytes 100
  245.7 45.9 %copy-start.1 = (bf16[16,26,128]{2,0,1:T(8,128)(2,1)S(1)}, bf16[16,26,128]{2,0,1:T(8,128)(2,1)}, u32[]{:S(2)}) copy-start(bf16[16,26,128]{2,0,1:T(8,128)(2,1)} %param.14) | copy-start | bytes 319492
  245.7 45.9 %copy-start.2 = (f32[16,128]{1,0:T(8,128)S(1)}, f32[16,128]{1,0:T(8,128)}, u32[]{:S(2)}) copy-start(f32[16,128]{1,0:T(8,128)} %param.16) | copy-start | bytes 24580
Sparse Core Ops, SparseCore 0:
  9.9 197.4 all-gather.1
  257.4 34.0 reduce-scatter.1
where the time goes:
time: 300 us
  waiting for transfers between devices  232 us (77%)
  local copies, waits for them, and re-layouts  34.5 us (12%)
  matrix products  16.1 us (5%)
  between operations  13.4 us (4%)
  other arithmetic  4.1 us (1%)
    all_gather x1, waiting for transfers between devices, local(): gathered = lax.all_gather(amplitudes, 'proc', axis=0, tiled=True)  198 us
    reduce_scatter x1, waiting for transfers between devices, local(): lax.psum_scatter(partial_value, 'rep', scatter_dimension=1, tiled=True)  33.6 us
    gather x1, local copies, waits for them, and re-layouts, local(): ladder_tiles = gathered[jnp.maximum(ladder_list, 0)]  19.3 us
    gather x1, local copies, waits for them, and re-layouts, local(): cycle_tiles = gathered[cycle_rows[:, 0, :]]  12.9 us
    dot_general x1, matrix products, local(): jnp.einsum('lsrk,lskc->lrc', ladder_tiles, ladder_ints[:, 0], preferred_e...  9.86 us
    dot_general x1, matrix products, local(): jnp.einsum('lsrk,lskc->lrc', cycle_tiles, cycle_ints[:, 0], preferred_ele...  6.06 us
  transfers between devices with their start and end apart: 2, of which 2 were waited for; matrix products, arithmetic and copies ran while one was open for 1% of the time, Pallas kernels for 0%

commit v1 on v0

--- a/solution.py
+++ b/solution.py
@@ -19,7 +19,9 @@
     replica = lax.axis_index("rep")
     proc_index = lax.axis_index("proc")
     tiles_dev, pair_rows, tile_width = amplitudes.shape
-    gathered = lax.all_gather(amplitudes, "proc", axis=0, tiled=True)
+    gathered = jnp.concatenate(
+        lax.all_to_all(jnp.stack([amplitudes] * lax.axis_size("proc")), "proc", 0, 0), axis=0
+    )
     ladder_list = ladder_rows[:, 0, :]
     usable = ladder_list >= 0
     ladder_tiles = gathered[jnp.maximum(ladder_list, 0)]

time: 300 us -> 786 us (2.62)
  waiting for transfers between devices: 232 us -> 697 us
  starting transfers between devices: 0.04 us -> 11.9 us
  local copies, waits for them, and re-layouts: 34.5 us -> 45 us
    all_to_all x0 -> x1, waiting for transfers between devices: none -> 628 us  [local(): lax.all_to_all(jnp.stack([amplitudes] * lax.axis_size('proc')), 'proc', 0...]
    all_gather x1 -> x0, waiting for transfers between devices: 198 us -> none  [local(): gathered = lax.all_gather(amplitudes, 'proc', axis=0, tiled=True)]
    reduce_scatter x1, waiting for transfers between devices: 33.6 us -> 69.4 us  [local(): lax.psum_scatter(partial_value, 'rep', scatter_dimension=1, tiled=True)]
    all_to_all x0 -> x1, starting transfers between devices: none -> 11.8 us  [local(): lax.all_to_all(jnp.stack([amplitudes] * lax.axis_size('proc')), 'proc', 0...]
    another operation x0 -> x1, local copies, waits for them, and re-layouts: none -> 10.5 us  [local(): jnp.stack([amplitudes] * lax.axis_size('proc'))]
  transfers between devices with their start and end apart: 2 -> 2, of which waited for: 2 -> 2; matrix products, arithmetic and copies ran while one was open for 1% -> 0% of each run, Pallas kernels for 0% -> 0%
where the time goes in v1:
time: 786 us
  waiting for transfers between devices  697 us (89%)
  local copies, waits for them, and re-layouts  45 us (6%)
  matrix products  16.1 us (2%)
  between operations  13.5 us (2%)
  starting transfers between devices  11.9 us (2%)
    all_to_all x1, waiting for transfers between devices, local(): lax.all_to_all(jnp.stack([amplitudes] * lax.axis_size('proc')), 'proc', 0...  628 us
    reduce_scatter x1, waiting for transfers between devices, local(): lax.psum_scatter(partial_value, 'rep', scatter_dimension=1, tiled=True)  69.4 us
    gather x1, local copies, waits for them, and re-layouts, local(): ladder_tiles = gathered[jnp.maximum(ladder_list, 0)]  19.3 us
  transfers between devices with their start and end apart: 2, of which 2 were waited for; matrix products, arithmetic and copies ran while one was open for 0% of the time, Pallas kernels for 0%

profile of v1, /device:TPU:2, one launch (start us, length us, event | category | flops | bytes accessed | tf_op | source)
XLA Modules:
  0.0 786.0 jit_solution(5117805349003620924)
XLA Ops:
  6.5 0.0 copy-start
  6.5 10.5 %stack.2 = bf16[32,16,208,128]{3,2,1,0:T(8,128)(2,1)} broadcast(bf16[16,208,128]{2,1,0:T(8,128)(2,1)} %param.9), dimensions={1,2,3} | broadcast | bytes 28114944 | tf_op jit(solution)/shard_map/stack | solution.py:23
  17.0 0.0 copy-start.4
  17.0 0.0 copy-start.2
  17.0 11.8 %all-to-all-start = ((bf16[32,16,208,128]{3,2,1,0:T(8,128)(2,1)}), bf16[32,16,208,128]{3,2,1,0:T(8,128)(2,1)}, u32[]{:S(2)}, u32[]{:S(2)}) async-start(bf16[32,16,208,128]{3,2,1,0:T(8,128)(2,1)} %stack.2), calls=%async_computation | async-start | bytes 54525952 | tf_op jit(solution)/shard_map/all_to_all | solution.py:23
  28.9 0.0 reduce-scatter.2.cloned.1.call-start
  28.9 0.0 copy-done.4
  28.9 0.1 copy.26
  29.0 0.1 reshape.96
  29.1 0.0 copy-done.2
  29.1 0.1 copy.25
  29.2 0.1 reshape.88
  29.3 0.1 copy.31
  29.4 628.1 %all-to-all-done = bf16[32,16,208,128]{3,2,1,0:T(8,128)(2,1)} async-done(((bf16[32,16,208,128]{3,2,1,0:T(8,128)(2,1)}), bf16[32,16,208,128]{3,2,1,0:T(8,128)(2,1)}, u32[]{:S(2)}, u32[]{:S(2)}) %all-to-all-start) | async-done | bytes 27263008 | tf_op jit(solution)/shard_map/all_to_all | solution.py:23
  657.5 12.9 %gather_fusion.1 = bf16[128,208,128]{2,1,0:T(8,128)(2,1)} fusion(bf16[512,208,128]{2,1,0:T(8,128)(2,1)} %bitcast.1, s32[1024]{0:T(1024)S(1)} %pad_clamp_fusion), kind=kCustom, calls=%fused_computation.1 | custom fusion | bytes 13632000 | tf_op jit(solution)/shard_map/gather | solution.py:34
  670.4 19.3 %gather_fusion = bf16[224,208,128]{2,1,0:T(8,128)(2,1)} fusion(bf16[512,208,128]{2,1,0:T(8,128)(2,1)} %bitcast.1, s32[1024]{0:T(1024)S(1)} %pad_clamp_fusion.1), kind=kCustom, calls=%fused_computation | custom fusion | bytes 23856000 | tf_op jit(solution)/shard_map/gather | solution.py:27
  689.7 6.0 fusion.5
  695.8 0.0 copy-start.5
  695.8 0.0 copy-start.1
  695.8 0.0 copy-start.3
  695.8 9.8 %bitcast_add_fusion = f32[16,208,128]{2,1,0:T(8,128)S(1)} fusion(f32[16,208,128,1]{2,1,3,0:T(8,128)S(1)} %fusion.5, bf16[16,1,14,128,128]{4,3,2,1,0:T(8,128)(2,1)} %param.11, bf16[16,14,208,128]{3,2,1,0:T(8,128)(2,1)} %bitcast.29, pred[16,14]{1,0:T(8,128)(4,1)S(1)} %bitcast.30), kind=kOutput, calls=%fused_computation.9 | convolution fusion | flops 1533116416 | bytes 22675680 | tf_op jit(solution)/shard_map/lsrk,lskc->lrc/dot_general | solution.py:31
  705.6 1.7 copy.27
  707.4 0.0 reduce-scatter.2.cloned.1.call-update
  707.4 0.0 copy-done.5
  707.4 0.2 reduce-window.8
  707.6 0.1 convert_reduce_fusion
  707.7 0.0 copy-done
  707.7 0.2 fusion.11
  707.9 0.1 constant_dynamic-slice_fusion
  707.9 0.1 copy.28
  708.0 69.4 %reduce-scatter.2.cloned.1.call-done = f32[16,26,128]{2,0,1:T(8,128)} async-done(((f32[16,208,128]{2,0,1:T(8,128)}), f32[16,26,128]{2,0,1:T(8,128)}) %reduce-scatter.2.cloned.1.call-update) | async-done | bytes 213008 | tf_op jit(solution)/shard_map/reduce_scatter | solution.py:39
  777.4 0.0 copy-done.1
  777.4 0.0 copy-done.3
  777.4 1.7 divide_convert_fusion
  (6 shorter events, 0.0 us)
Async XLA Ops:
  6.5 701.1 %copy-start = (f32[8,208]{1,0:T(8,128)S(1)}, f32[8,208]{1,0:T(8,128)}, u32[]{:S(2)}) copy-start(f32[8,208]{1,0:T(8,128)} %param.15) | copy-start | bytes 19972
  17.0 11.9 %copy-start.4 = (s32[16,1,8]{0,2,1:T(8,128)S(1)}, s32[16,1,8]{0,2,1:T(8,128)}, u32[]{:S(2)}) copy-start(s32[16,1,8]{0,2,1:T(8,128)} %param.12) | copy-start | bytes 1540
  17.0 12.1 %copy-start.2 = (s32[16,1,14]{0,1,2:T(1,128)S(1)}, s32[16,1,14]{0,1,2:T(1,128)}, u32[]{:S(2)}) copy-start(s32[16,1,14]{0,1,2:T(1,128)} %param.10) | copy-start | bytes 2692
  17.0 640.4 %all-to-all-start = ((bf16[32,16,208,128]{3,2,1,0:T(8,128)(2,1)}), bf16[32,16,208,128]{3,2,1,0:T(8,128)(2,1)}, u32[]{:S(2)}, u32[]{:S(2)}) async-start(bf16[32,16,208,128]{3,2,1,0:T(8,128)(2,1)} %stack.2), calls=%async_computation | async-start | bytes 54525952 | tf_op jit(solution)/shard_map/all_to_all | solution.py:23
  28.9 748.5 %reduce-scatter.2.cloned.1.call-start = ((), (), s32[]{:S(2)}) async-start(), calls=%async_computation.2 | async-start | bytes 1916928 | tf_op jit(solution)/shard_map/reduce_scatter | solution.py:39
  695.8 11.6 %copy-start.5 = (s32[8]{0:T(128)S(1)}, s32[8]{0:T(128)}, u32[]{:S(2)}) copy-start(s32[8]{0:T(128)} %param.17) | copy-start | bytes 100
  695.8 81.6 %copy-start.1 = (bf16[16,26,128]{2,0,1:T(8,128)(2,1)S(1)}, bf16[16,26,128]{2,0,1:T(8,128)(2,1)}, u32[]{:S(2)}) copy-start(bf16[16,26,128]{2,0,1:T(8,128)(2,1)} %param.14) | copy-start | bytes 319492
  695.8 81.6 %copy-start.3 = (f32[16,128]{1,0:T(8,128)S(1)}, f32[16,128]{1,0:T(8,128)}, u32[]{:S(2)}) copy-start(f32[16,128]{1,0:T(8,128)} %param.16) | copy-start | bytes 24580
Sparse Core Ops, SparseCore 0:
  707.5 69.8 reduce-scatter.1
